TPU v7x, 32 devices: a whole 2x2x4 slice. The times are simulated.
32 devices in a mesh: tok: 16 (over z, y, x), head: 2 (over core).
Axes of the slice: x: 2, y: 2, z: 4, core: 2. Of those that a mesh axis runs over, the one named last changes fastest.
Arguments:
- queries: bfloat16 [2, 4096, 512], P('head', 'tok'), may hold values from -6 to 6
- key_rows: bfloat16 [2, 4096, 512], P('head', 'tok'), may hold values from -6 to 6
- value_rows: bfloat16 [2, 4096, 512], P('head', 'tok'), may hold values from -6 to 6
- step_rates: float32 [2, 4096], P('head', 'tok'), may hold values from 0.1 to 1
- w_gate: bfloat16 [2, 512, 512], P('head'), may hold values from -0.25 to 0.25
- w_up: bfloat16 [2, 512, 512], P('head'), may hold values from -0.25 to 0.25
- w_down: bfloat16 [2, 512, 512], P('head'), may hold values from -0.25 to 0.25
- out_gain: float32 [2, 512], P('head'), may hold values from 0.1 to 1.9
- cotangent: bfloat16 [2, 4096, 512], P('head', 'tok'), may hold values from -6 to 6
Outputs:
- grad_queries: bfloat16 [2, 4096, 512], P('head', 'tok')
- grad_keys: bfloat16 [2, 4096, 512], P('head', 'tok')
- grad_values: bfloat16 [2, 4096, 512], P('head', 'tok')
- grad_gate: float32 [2, 512, 512], P('head', 'tok')
- grad_up: float32 [2, 512, 512], P('head', 'tok')
- grad_down: float32 [2, 512, 512], P('head', 'tok')
All inputs are finite; a program needn't handle non-finite values.
Results may differ from a plain program's by a relative error of at most 0.03.
Values sent between devices are 32-bit elements; how exact they have to be, the bound alone decides.
A program may use at most 128 MiB of HBM per device.

v0:
```python
import jax
import jax.numpy as jnp
from jax import lax
from jax.sharding import PartitionSpec as P

NS_STEPS = 3
coef_first = 3.4445
coef_second = -4.775
coef_third = 2.0315
inner_step = 0.5


def contract_rows(first_op, second_op):
    return lax.dot_general(
        first_op, second_op, (((0,), (0,)), ((), ())), preferred_element_type=jnp.float32
    )


def contract_cols(first_op, second_op):
    return lax.dot_general(
        first_op, second_op, (((1,), (1,)), ((), ())), preferred_element_type=jnp.float32
    )


def silu_parts(pre_gate):
    sigma_gate = jax.nn.sigmoid(pre_gate)
    act_gate = pre_gate * sigma_gate
    slope_gate = sigma_gate * (1.0 + pre_gate * (1.0 - sigma_gate))
    return (act_gate, slope_gate, sigma_gate)


def orthogonalize(matrix):
    current = matrix / jnp.sqrt(jnp.sum(matrix * matrix) + 1e-06)
    for iteration in range(NS_STEPS):
        narrow = current.astype(jnp.bfloat16)
        gram_matrix = contract_cols(narrow, narrow)
        gram_low = gram_matrix.astype(jnp.bfloat16)
        poly_term = (
            coef_second * gram_matrix
            + coef_third * jnp.dot(gram_low, gram_low, preferred_element_type=jnp.float32)
        ).astype(jnp.bfloat16)
        current = coef_first * current + jnp.dot(
            poly_term, narrow, preferred_element_type=jnp.float32
        )
    return current


def orthogonalize_all(grad_triple):
    mapped = jax.vmap(orthogonalize)
    return (mapped(grad_triple[0]), mapped(grad_triple[1]), mapped(grad_triple[2]))


def key_forward(w_gate, w_up, w_down, key_rows, value_rows, step_rates):
    key_gate = jnp.dot(key_rows, w_gate, preferred_element_type=jnp.float32)
    key_up = jnp.dot(key_rows, w_up, preferred_element_type=jnp.float32)
    act_gate, slope_gate, sigma_gate = silu_parts(key_gate)
    key_mixed = (act_gate * key_up).astype(jnp.bfloat16)
    target = (-step_rates[:, None] * value_rows).astype(jnp.bfloat16)
    key_mid = contract_cols(target, w_down)
    key_dgate = (key_mid * key_up * slope_gate).astype(jnp.bfloat16)
    key_dup = (key_mid * act_gate).astype(jnp.bfloat16)
    inner_grads = (
        contract_rows(key_rows, key_dgate),
        contract_rows(key_rows, key_dup),
        contract_rows(key_mixed, target),
    )
    stored = (
        key_gate,
        key_up,
        act_gate,
        slope_gate,
        sigma_gate,
        key_mixed,
        target,
        key_mid,
        key_dgate,
        key_dup,
    )
    return (inner_grads, stored)


def key_backward(w_gate, w_up, w_down, key_rows, step_rates, stored, back_a, back_b, back_c):
    (
        key_gate,
        key_up,
        act_gate,
        slope_gate,
        sigma_gate,
        key_mixed,
        target,
        key_mid,
        key_dgate,
        key_dup,
    ) = stored
    cot_a = back_a.astype(jnp.bfloat16)
    cot_b = back_b.astype(jnp.bfloat16)
    cot_c = back_c.astype(jnp.bfloat16)
    back_gate = jnp.dot(key_rows, cot_a, preferred_element_type=jnp.float32)
    back_up = jnp.dot(key_rows, cot_b, preferred_element_type=jnp.float32)
    back_mixed = contract_cols(target, cot_c)
    back_target = jnp.dot(key_mixed, cot_c, preferred_element_type=jnp.float32)
    curve_gate = sigma_gate * (1.0 - sigma_gate) * (2.0 + key_gate * (1.0 - 2.0 * sigma_gate))
    back_mid = (back_gate * key_up * slope_gate + back_up * act_gate).astype(jnp.bfloat16)
    gate_back = (
        back_gate * key_mid * key_up * curve_gate
        + back_up * key_mid * slope_gate
        + back_mixed * key_up * slope_gate
    ).astype(jnp.bfloat16)
    up_back = (back_gate * key_mid * slope_gate + back_mixed * act_gate).astype(jnp.bfloat16)
    key_grad = (
        contract_cols(key_dgate, cot_a)
        + contract_cols(key_dup, cot_b)
        + contract_cols(gate_back, w_gate)
        + contract_cols(up_back, w_up)
    )
    value_sum = back_target + jnp.dot(back_mid, w_down, preferred_element_type=jnp.float32)
    value_grad = (-step_rates[:, None] * value_sum).astype(jnp.bfloat16)
    weight_terms = jnp.concatenate(
        [
            contract_rows(key_rows, gate_back),
            contract_rows(key_rows, up_back),
            contract_rows(back_mid, target),
        ],
        axis=1,
    )
    return (key_grad.astype(jnp.bfloat16), value_grad, weight_terms)


def query_forward(new_gate, new_up, new_down, queries):
    query_gate = jnp.dot(queries, new_gate, preferred_element_type=jnp.float32)
    query_up = jnp.dot(queries, new_up, preferred_element_type=jnp.float32)
    act_gate, slope_gate, sigma_gate = silu_parts(query_gate)
    query_mixed = (act_gate * query_up).astype(jnp.bfloat16)
    output = jnp.dot(query_mixed, new_down, preferred_element_type=jnp.float32)
    return (output, (query_up, act_gate, slope_gate, query_mixed))


def query_backward(new_gate, new_up, new_down, queries, stored, grad_output):
    query_up, act_gate, slope_gate, query_mixed = stored
    query_mid = contract_cols(grad_output, new_down)
    query_dgate = (query_mid * query_up * slope_gate).astype(jnp.bfloat16)
    query_dup = (query_mid * act_gate).astype(jnp.bfloat16)
    query_grad = (contract_cols(query_dgate, new_gate) + contract_cols(query_dup, new_up)).astype(
        jnp.bfloat16
    )
    weight_terms = jnp.concatenate(
        [
            contract_rows(queries, query_dgate),
            contract_rows(queries, query_dup),
            contract_rows(query_mixed, grad_output),
        ],
        axis=1,
    )
    return (query_grad, weight_terms)


def local(queries, key_rows, value_rows, step_rates, w_gate, w_up, w_down, out_gain, cotangent):
    head_size = w_gate.shape[2]
    local_grads, stored = jax.vmap(key_forward)(
        w_gate, w_up, w_down, key_rows, value_rows, step_rates
    )
    inner_grads = lax.psum((local_grads[0], local_grads[1], local_grads[2]), "tok")
    unitary, ns_back = jax.vjp(orthogonalize_all, inner_grads)
    new_gate = (w_gate - inner_step * unitary[0]).astype(jnp.bfloat16)
    new_up = (w_up - inner_step * unitary[1]).astype(jnp.bfloat16)
    new_down = (w_down - inner_step * unitary[2]).astype(jnp.bfloat16)
    output, query_stored = jax.vmap(query_forward)(new_gate, new_up, new_down, queries)
    full_width = queries.shape[0] * lax.axis_size("head") * head_size
    squares_local = jnp.sum(output * output, axis=(0, 2))
    gain_wide = out_gain[:, None, :]
    squares, aligned = lax.psum(
        (squares_local, jnp.sum(cotangent * gain_wide * output, axis=(0, 2))), "head"
    )
    inverse_rms = lax.rsqrt(squares / full_width + 1e-05)
    grad_output = (
        gain_wide * cotangent * inverse_rms[None, :, None]
        - output * (aligned * inverse_rms * inverse_rms * inverse_rms / full_width)[None, :, None]
    ).astype(jnp.bfloat16)
    query_grad, query_terms = jax.vmap(query_backward)(
        new_gate, new_up, new_down, queries, query_stored, grad_output
    )
    share_rows = head_size // lax.axis_size("tok")
    query_whole = lax.psum(query_terms, "tok")
    query_share = lax.dynamic_slice_in_dim(
        query_whole, lax.axis_index("tok") * share_rows, share_rows, 1
    )
    outer_back = (
        -inner_step * query_whole[:, :, :head_size],
        -inner_step * query_whole[:, :, head_size : 2 * head_size],
        -inner_step * query_whole[:, :, 2 * head_size :],
    )
    back_triple = ns_back(outer_back)[0]
    key_grad, value_grad, key_terms = jax.vmap(key_backward)(
        w_gate,
        w_up,
        w_down,
        key_rows,
        step_rates,
        stored,
        back_triple[0],
        back_triple[1],
        back_triple[2],
    )
    key_share = lax.psum_scatter(key_terms, "tok", scatter_dimension=1, tiled=True)
    weight_share = query_share + key_share
    return (
        query_grad,
        key_grad,
        value_grad,
        weight_share[:, :, :head_size],
        weight_share[:, :, head_size : 2 * head_size],
        weight_share[:, :, 2 * head_size :],
    )


def solution(mesh):
    in_specs = (
        P("head", "tok", None),
        P("head", "tok", None),
        P("head", "tok", None),
        P("head", "tok"),
        P("head", None, None),
        P("head", None, None),
        P("head", None, None),
        P("head", None),
        P("head", "tok", None),
    )
    out_specs = (
        P("head", "tok", None),
        P("head", "tok", None),
        P("head", "tok", None),
        P("head", "tok", None),
        P("head", "tok", None),
        P("head", "tok", None),
    )
    return jax.shard_map(local, mesh=mesh, in_specs=in_specs, out_specs=out_specs, check_vma=False)
```

profile of v0, /device:TPU:0, one launch (start us, length us, event | category | flops | bytes accessed | tf_op | source)
XLA Modules:
  0.0 571.0 jit_solution(9727249518634274139)
XLA Ops:
  8.1 1.3 fusion.266
  9.5 1.6 fusion.272
  11.1 2.4 multiply_convert_fusion.2
  13.6 1.3 convolution_bitcast_fusion.8
  14.9 1.4 convolution_bitcast_fusion.7
  16.3 1.4 convolution_bitcast_fusion.6
  21.0 146.9 %all-reduce.11.cloned.1.call-done = (f32[1,512,512]{1,2,0:T(8,128)}, f32[1,512,512]{1,2,0:T(8,128)}, f32[1,512,512]{1,2,0:T(8,128)}) async-done(((f32[1,512,512]{1,2,0:T(8,128)}, f32[1,512,512]{1,2,0:T(8,128)}, f32[1,512,512]{1,2,0:T(8,128)}), (f32[1,512,512]{1,2,0:T(8,128)}, f32[1,512,512]{1,2,0:T(8,128)}, f32[1,512,512]{1,2,0:T(8,128)})) %all-reduce.11.cloned.1.call-update) | async-done | bytes 3145744 | tf_op jit(solution)/shard_map/psum | solution.py:162
  167.9 2.1 multiply_reduce_fusion.5
  170.7 2.2 fusion.263
  198.0 2.5 all-reduce.2
  203.1 1.8 multiply_convert_fusion
  206.0 2.0 pad_maximum_fusion
  208.5 145.7 %all-reduce.7.cloned.1.call-done = f32[1,512,1536]{1,2,0:T(8,128)} async-done(((f32[1,512,1536]{1,2,0:T(8,128)}), f32[1,512,1536]{1,2,0:T(8,128)}) %all-reduce.7.cloned.1.call-update) | async-done | bytes 3145744 | tf_op jit(solution)/shard_map/psum | solution.py:183
  354.2 1.8 convolution_convert_fusion.52
  356.1 1.7 fusion.39
  383.9 2.2 multiply_reduce_fusion.2
  386.7 1.9 fusion.49
  388.6 2.0 fusion.103
  391.9 2.1 multiply_reduce_fusion.1
  394.7 3.0 fusion.172
  407.2 5.7 copy.106
  416.1 2.0 fusion.161
  421.6 137.6 %all-reduce.9.cloned.1.call-done = f32[1,512,1536]{2,0,1:T(1,128)} async-done(((f32[1,512,1536]{2,0,1:T(1,128)}), f32[1,512,1536]{2,0,1:T(1,128)}) %all-reduce.9.cloned.1.call-update) | async-done | bytes 3145744
  560.4 1.4 dynamic-slice_add_fusion
  (329 shorter events, 76.0 us)
Async XLA Ops:
  7.2 160.8 %all-reduce.11.cloned.1.call-start = ((), (), s32[]{:S(2)}) async-start(), calls=%async_computation.2 | async-start | bytes 6291456 | tf_op jit(solution)/shard_map/psum | solution.py:162
  9.5 5.4 copy-start.89
  11.1 5.2 copy-start.91
  11.1 5.2 copy-start.46
  16.3 3.7 copy-start.29
  17.8 336.4 %all-reduce.7.cloned.1.call-start = ((), (), s32[]{:S(2)}) async-start(), calls=%async_computation | async-start | bytes 6291456 | tf_op jit(solution)/shard_map/psum | solution.py:183
  193.0 3.1 copy-start.62
  200.5 4.4 copy-start.49
  208.0 351.1 %all-reduce.9.cloned.1.call-start = ((), (), s32[]{:S(2)}) async-start(), calls=%async_computation.1 | async-start | bytes 6291456
  354.2 3.6 copy-start.19
  354.2 4.1 copy-start.1
  354.2 4.1 copy-start.71
  386.7 4.0 copy-start.102
  394.7 4.2 copy-start.38
  394.7 4.2 copy-start.72
  412.9 3.2 copy-start.51
  412.9 5.3 copy-start.25
  412.9 5.3 copy-start.78
  412.9 5.6 copy-start.53
  412.9 5.6 copy-start.76
  412.9 5.9 %copy-start.21 = (bf16[1,512,512]{2,1,0:T(8,128)(2,1)S(1)}, bf16[1,512,512]{2,1,0:T(8,128)(2,1)}, u32[]{:S(2)}) copy-start(bf16[1,512,512]{2,1,0:T(8,128)(2,1)} %param.13) | copy-start | bytes 1572868
  414.8 4.0 copy-start.81
  416.1 3.1 copy-start.55
  416.1 3.1 copy-start.87
  (85 other events, 140.0 us)
Sparse Core Ops, SparseCore 0:
  17.9 149.9 all-reduce.10
  208.2 146.0 all-reduce.6
  413.0 146.1 all-reduce.8
where the time goes:
time: 582 us; the launch traced here: 571 us
  waiting for transfers between devices  430 us (74%)
  matrix products  79.5 us (14%)
  local copies, waits for them, and re-layouts  24.8 us (4%)
  between operations  20.8 us (4%)
  other arithmetic  12.9 us (2%)
    psum x1, waiting for transfers between devices, local(): lax.psum((local_grads[0], local_grads[1], local_grads[2]), 'tok')  147 us
    psum x1, waiting for transfers between devices, local(): query_whole = lax.psum(query_terms, 'tok')  146 us
    unnamed x4, waiting for transfers between devices  138 us
    dot_general x36, matrix products, contract_cols(): lax.dot_general(first_op, second_op, (((1,), (1,)), ((), ())), preferred_...  27.5 us
    unnamed x220, local copies, waits for them, and re-layouts  18.8 us
    dot_general x27, matrix products, orthogonalize(): jnp.dot(gram_low, gram_low, preferred_element_type=jnp.float32)  18.8 us
    dot_general x27, matrix products, orthogonalize(): jnp.dot(poly_term, narrow, preferred_element_type=jnp.float32)  17.2 us
  transfers between devices with their start and end apart: 3, of which 3 were waited for; matrix products, arithmetic and copies ran while one was open for 2% of the time, Pallas kernels for 0%

commit v1 on v0

--- a/solution.py
+++ b/solution.py
@@ -180,7 +180,11 @@
         new_gate, new_up, new_down, queries, query_stored, grad_output
     )
     share_rows = head_size // lax.axis_size("tok")
-    query_whole = lax.psum(query_terms, "tok")
+    query_whole = query_terms
+    for hop in (1, 2, 4, 8):
+        query_whole = query_whole + lax.ppermute(
+            query_whole, "tok", [(dev, dev ^ hop) for dev in range(16)]
+        )
     query_share = lax.dynamic_slice_in_dim(
         query_whole, lax.axis_index("tok") * share_rows, share_rows, 1
     )

time: 582 us -> 792 us (1.36)
  waiting for transfers between devices: 430 us -> 621 us
    ppermute x0 -> x4, waiting for transfers between devices: none -> 338 us  [local(): lax.ppermute(query_whole, 'tok', [(dev, dev ^ hop) for dev in range(16)])]
    psum x1 -> x0, waiting for transfers between devices: 146 us -> none  [local(): query_whole = lax.psum(query_terms, 'tok')]
    unnamed x4 -> x3, waiting for transfers between devices: 138 us -> 136 us
  transfers between devices with their start and end apart: 3 -> 6, of which waited for: 3 -> 6; matrix products, arithmetic and copies ran while one was open for 2% -> 2% of each run, Pallas kernels for 0% -> 0%
where the time goes in v1:
time: 792 us; the launch traced here: 781 us
  waiting for transfers between devices  621 us (78%)
  matrix products  78.7 us (10%)
  local copies, waits for them, and re-layouts  31.4 us (4%)
  between operations  21.1 us (3%)
  other arithmetic  19.9 us (3%)
    ppermute x4, waiting for transfers between devices, local(): lax.ppermute(query_whole, 'tok', [(dev, dev ^ hop) for dev in range(16)])  338 us
    psum x1, waiting for transfers between devices, local(): lax.psum((local_grads[0], local_grads[1], local_grads[2]), 'tok')  147 us
    unnamed x3, waiting for transfers between devices  136 us
    dot_general x36, matrix products, contract_cols(): lax.dot_general(first_op, second_op, (((1,), (1,)), ((), ())), preferred_...  30.5 us
    unnamed x220, local copies, waits for them, and re-layouts  20.7 us
    dot_general x27, matrix products, orthogonalize(): jnp.dot(gram_low, gram_low, preferred_element_type=jnp.float32)  17.5 us
    dot_general x27, matrix products, orthogonalize(): jnp.dot(poly_term, narrow, preferred_element_type=jnp.float32)  15.8 us
  transfers between devices with their start and end apart: 6, of which 6 were waited for; matrix products, arithmetic and copies ran while one was open for 2% of the time, Pallas kernels for 0%

profile of v1, /device:TPU:0, one launch (start us, length us, event | category | flops | bytes accessed | tf_op | source)
XLA Modules:
  0.0 780.9 jit_solution(13507986330791475253)
XLA Ops:
  9.5 1.6 fusion.278
  11.2 2.4 multiply_convert_fusion.2
  20.7 147.1 %all-reduce.8.cloned.1.call-done = (f32[1,512,512]{1,2,0:T(8,128)}, f32[1,512,512]{1,2,0:T(8,128)}, f32[1,512,512]{1,2,0:T(8,128)}) async-done(((f32[1,512,512]{1,2,0:T(8,128)}, f32[1,512,512]{1,2,0:T(8,128)}, f32[1,512,512]{1,2,0:T(8,128)}), (f32[1,512,512]{1,2,0:T(8,128)}, f32[1,512,512]{1,2,0:T(8,128)}, f32[1,512,512]{1,2,0:T(8,128)})) %all-reduce.8.cloned.1.call-update) | async-done | bytes 3145744 | tf_op jit(solution)/shard_map/psum | solution.py:162
  167.8 2.1 multiply_reduce_fusion.5
  170.6 2.2 fusion.269
  199.6 2.6 all-reduce.2
  206.7 68.7 %collective-permute-done = f32[1,512,1536]{1,2,0:T(8,128)S(1)} collective-permute-done((f32[1,512,1536]{1,2,0:T(8,128)S(1)}, f32[1,512,1536]{1,2,0:T(8,128)S(1)}, u32[]{:S(2)}, u32[]{:S(2)}) %collective-permute-start) | collective-permute-done | bytes 3145760 | tf_op jit(solution)/shard_map/ppermute | solution.py:185
  277.7 67.8 %collective-permute-done.1 = f32[1,512,1536]{1,2,0:T(8,128)S(1)} collective-permute-done((f32[1,512,1536]{1,2,0:T(8,128)S(1)}, f32[1,512,1536]{1,2,0:T(8,128)S(1)}, u32[]{:S(2)}, u32[]{:S(2)}) %collective-permute-start.1) | collective-permute-done | bytes 3145760 | tf_op jit(solution)/shard_map/ppermute | solution.py:185
  347.2 67.7 %collective-permute-done.2 = f32[1,512,1536]{1,2,0:T(8,128)S(1)} collective-permute-done((f32[1,512,1536]{1,2,0:T(8,128)S(1)}, f32[1,512,1536]{1,2,0:T(8,128)S(1)}, u32[]{:S(2)}, u32[]{:S(2)}) %collective-permute-start.2) | collective-permute-done | bytes 3145760 | tf_op jit(solution)/shard_map/ppermute | solution.py:185
  417.5 134.2 %collective-permute-done.3 = f32[1,512,1536]{1,2,0:T(8,128)} collective-permute-done((f32[1,512,1536]{1,2,0:T(8,128)S(1)}, f32[1,512,1536]{1,2,0:T(8,128)}, u32[]{:S(2)}, u32[]{:S(2)}) %collective-permute-start.3) | collective-permute-done | bytes 3145760 | tf_op jit(solution)/shard_map/ppermute | solution.py:185
  551.7 3.6 add.198
  583.2 2.1 multiply_reduce_fusion.2
  586.0 2.0 fusion.49
  588.0 2.0 fusion.103
  591.2 2.1 multiply_reduce_fusion.1
  594.0 3.7 fusion.166
  601.1 2.1 multiply_reduce_fusion
  603.9 2.0 fusion.168
  609.5 1.9 pad_maximum_fusion.1
  611.4 8.6 %copy.106 = f32[1,512,1536]{2,0,1:T(1,128)} copy(f32[1,512,1536]{1,2,0:T(8,128)} %pad_maximum_fusion.1) | data formatting | bytes 6291456 | tf_op jit(solution)/shard_map/vmap()/concatenate | solution.py:118
  623.5 2.3 fusion.155
  630.3 135.9 %all-reduce.6.cloned.1.call-done = f32[1,512,1536]{2,0,1:T(1,128)} async-done(((f32[1,512,1536]{2,0,1:T(1,128)}), f32[1,512,1536]{2,0,1:T(1,128)}) %all-reduce.6.cloned.1.call-update) | async-done | bytes 3145744
  766.2 1.6 constant_dynamic-slice_fusion
  767.8 2.1 copy.107
  (338 shorter events, 91.2 us)
Async XLA Ops:
  7.2 160.6 %all-reduce.8.cloned.1.call-start = ((), (), s32[]{:S(2)}) async-start(), calls=%async_computation.1 | async-start | bytes 6291456 | tf_op jit(solution)/shard_map/psum | solution.py:162
  9.5 5.4 copy-start.90
  11.1 5.0 copy-start.92
  11.1 5.1 copy-start.52
  17.6 748.6 %all-reduce.6.cloned.1.call-start = ((), (), s32[]{:S(2)}) async-start(), calls=%async_computation | async-start | bytes 6291456
  177.3 18.1 %copy-start.5 = (f32[1,512,512]{1,2,0:T(8,128)}, f32[1,512,512]{1,2,0:T(8,128)S(1)}, u32[]{:S(2)}) copy-start(f32[1,512,512]{1,2,0:T(8,128)S(1)} %fusion.10) | copy-start | bytes 3145732
  186.1 10.3 %copy-start.3 = (f32[1,512,512]{1,2,0:T(8,128)}, f32[1,512,512]{1,2,0:T(8,128)S(1)}, u32[]{:S(2)}) copy-start(f32[1,512,512]{1,2,0:T(8,128)S(1)} %fusion.15) | copy-start | bytes 3145732
  194.4 4.0 copy-start.1
  205.2 70.2 %collective-permute-start = (f32[1,512,1536]{1,2,0:T(8,128)S(1)}, f32[1,512,1536]{1,2,0:T(8,128)S(1)}, u32[]{:S(2)}, u32[]{:S(2)}) collective-permute-start(f32[1,512,1536]{1,2,0:T(8,128)S(1)} %pad_maximum_fusion), channel_id=1, source_target_pairs={{0,2},{2,0},{4,6},{6,4},{8,10},{10,8},{12,14},{14,12},{16,18},{18,... | collective-permute-start | bytes 9437192 | tf_op jit(solution)/shard_map/ppermute | solution.py:185
  276.2 69.4 %collective-permute-start.1 = (f32[1,512,1536]{1,2,0:T(8,128)S(1)}, f32[1,512,1536]{1,2,0:T(8,128)S(1)}, u32[]{:S(2)}, u32[]{:S(2)}) collective-permute-start(f32[1,512,1536]{1,2,0:T(8,128)S(1)} %fusion.409), channel_id=1, source_target_pairs={{0,4},{2,6},{4,0},{6,2},{8,12},{10,14},{12,8},{14,10},{16,20},{18,... | collective-permute-start | bytes 9437192 | tf_op jit(solution)/shard_map/ppermute | solution.py:185
  346.3 68.5 %collective-permute-start.2 = (f32[1,512,1536]{1,2,0:T(8,128)S(1)}, f32[1,512,1536]{1,2,0:T(8,128)S(1)}, u32[]{:S(2)}, u32[]{:S(2)}) collective-permute-start(f32[1,512,1536]{1,2,0:T(8,128)S(1)} %add.196), channel_id=1, source_target_pairs={{0,8},{2,10},{4,12},{6,14},{8,0},{10,2},{12,4},{14,6},{16,24},{18,... | collective-permute-start | bytes 9437192 | tf_op jit(solution)/shard_map/ppermute | solution.py:185
  415.6 136.1 %collective-permute-start.3 = (f32[1,512,1536]{1,2,0:T(8,128)S(1)}, f32[1,512,1536]{1,2,0:T(8,128)}, u32[]{:S(2)}, u32[]{:S(2)}) collective-permute-start(f32[1,512,1536]{1,2,0:T(8,128)S(1)} %add.197), channel_id=1, source_target_pairs={{0,16},{2,18},{4,20},{6,22},{8,24},{10,26},{12,28},{14,30},{16,0},... | collective-permute-start | bytes 9437192 | tf_op jit(solution)/shard_map/ppermute | solution.py:185
  417.5 137.8 %copy-start.6 = (f32[1,512,512]{1,2,0:T(8,128)S(1)}, f32[1,512,512]{1,2,0:T(8,128)}, u32[]{:S(2)}) copy-start(f32[1,512,512]{1,2,0:T(8,128)} %copy-done.5) | copy-start | bytes 3145732
  585.9 4.0 copy-start.42
  585.9 4.0 copy-start.102
  594.0 4.8 copy-start.44
  594.0 4.8 copy-start.75
  621.9 3.9 copy-start.30
  621.9 5.3 copy-start.63
  621.9 5.3 copy-start.79
  621.9 5.6 copy-start.27
  621.9 5.6 copy-start.83
  623.5 4.4 copy-start.65
  623.5 4.4 copy-start.89
  (88 other events, 159.3 us)
Sparse Core Ops, SparseCore 0:
  17.7 149.9 all-reduce.7
  620.1 146.0 all-reduce.5
